TPU v7x, 32 devices: a whole 2x2x4 slice. The times are simulated.
32 devices in a mesh: dp: 2 (over y), ctx: 4 (over x, core), tensor: 4 (over z).
Axes of the slice: x: 2, y: 2, z: 4, core: 2. Of those that a mesh axis runs over, the one named last changes fastest.
Arguments:
- hidden: bfloat16 [4, 1024, 2048], P('dp', 'ctx'), may hold values from -6 to 6
- cotangent: bfloat16 [4, 1024, 2048], P('dp', 'ctx'), may hold values from -6 to 6
- segment_ids: int32 [4, 1024], P('dp', 'ctx'), may hold values from 0 to 5, never falling along the last dimension, each value on 1 to 800 neighbouring positions
- attn_gain: bfloat16 [2048], P(('dp', 'ctx')), may hold values from 0.5 to 1.5
- w_query: bfloat16 [2048, 2048], P(('dp', 'ctx'), 'tensor'), may hold values from -0.125 to 0.125
- key_matrix: bfloat16 [2048, 256], P(('dp', 'ctx'), 'tensor'), may hold values from -0.125 to 0.125
- value_matrix: bfloat16 [2048, 256], P(('dp', 'ctx'), 'tensor'), may hold values from -0.125 to 0.125
- w_out: bfloat16 [2048, 2048], P('tensor', ('dp', 'ctx')), may hold values from -1 to 1
- mlp_gain: bfloat16 [2048], P(('dp', 'ctx')), may hold values from 0.5 to 1.5
- w_gate: bfloat16 [2048, 5632], P(('dp', 'ctx'), 'tensor'), may hold values from -0.125 to 0.125
- w_up: bfloat16 [2048, 5632], P(('dp', 'ctx'), 'tensor'), may hold values from -0.125 to 0.125
- w_down: bfloat16 [5632, 2048], P('tensor', ('dp', 'ctx')), may hold values from -0.078125 to 0.078125
Outputs:
- layer_out: bfloat16 [4, 1024, 2048], P('dp', 'ctx')
- d_hidden: float32 [4, 1024, 2048], P('dp', 'ctx')
- grad_attn_gain: float32 [2048], P(('dp', 'ctx'))
- grad_query: float32 [2048, 2048], P(('dp', 'ctx'), 'tensor')
- grad_key: float32 [2048, 256], P(('dp', 'ctx'), 'tensor')
- grad_value: float32 [2048, 256], P(('dp', 'ctx'), 'tensor')
- grad_out: float32 [2048, 2048], P('tensor', ('dp', 'ctx'))
- grad_mlp_gain: float32 [2048], P(('dp', 'ctx'))
- grad_gate: float32 [2048, 5632], P(('dp', 'ctx'), 'tensor')
- grad_up: float32 [2048, 5632], P(('dp', 'ctx'), 'tensor')
- grad_down: float32 [5632, 2048], P('tensor', ('dp', 'ctx'))
Inputs may be any that keep to these rules, and one draw needn't show every extreme that they name: `segment_ids`: along each sequence the ids never fall, every id appears, each document holds 1 to 800 tokens, and one holds exactly 800.
All inputs are finite; a program needn't handle non-finite values.
Results may differ from a plain program's by a relative error of at most 0.013.
Values may be sent and summed in bfloat16 or wider, within the bound.
No kernel may reach another device: no remote copies, remote signals or barrier semaphores. Data moves between devices by JAX's collectives and lax.ppermute only.
A program may use at most 192 MiB of HBM per device.

v0:
```python
import jax
import jax.numpy as jnp
from jax import lax
from jax.sharding import PartitionSpec as P

MB = 2
EPSILON = 1e-05
THETA = 10000.0
NEG_FILL = -1e30


def inv_rms(values):
    return lax.rsqrt(jnp.mean(values * values, axis=-1, keepdims=True) + EPSILON)


def angles_for(positions, head_size):
    freq_index = jnp.arange(head_size // 2, dtype=jnp.float32)
    inverse = jnp.power(jnp.float32(THETA), -2.0 * freq_index / head_size)
    angle_table = positions.astype(jnp.float32)[:, None] * inverse[None, :]
    return (jnp.cos(angle_table), jnp.sin(angle_table))


def rotary(vectors, cosine, sine_table):
    half_size = vectors.shape[-1] // 2
    front_half = vectors[..., :half_size]
    back_half = vectors[..., half_size:]
    return jnp.concatenate(
        [
            front_half * cosine - back_half * sine_table,
            back_half * cosine + front_half * sine_table,
        ],
        axis=-1,
    )


def norm_back(grad_normed, source, inv_scale, gain_full):
    normalized = source * inv_scale
    scaled = grad_normed * gain_full
    middle = jnp.mean(scaled * normalized, axis=-1, keepdims=True)
    gain_term = jnp.sum(grad_normed * normalized, axis=(0, 1))
    return (inv_scale * (scaled - normalized * middle), gain_term)


def collect(shards):
    return (
        lax.all_gather(shards[0], ("dp", "ctx"), axis=0, tiled=True),
        lax.all_gather(shards[1], ("dp", "ctx"), axis=0, tiled=True),
        lax.all_gather(shards[2], ("dp", "ctx"), axis=0, tiled=True),
        lax.all_gather(shards[3], ("dp", "ctx"), axis=0, tiled=True),
        lax.all_gather(shards[4], ("dp", "ctx"), axis=1, tiled=True),
        lax.all_gather(shards[5], ("dp", "ctx"), axis=0, tiled=True),
        lax.all_gather(shards[6], ("dp", "ctx"), axis=0, tiled=True),
        lax.all_gather(shards[7], ("dp", "ctx"), axis=0, tiled=True),
        lax.all_gather(shards[8], ("dp", "ctx"), axis=1, tiled=True),
    )


def contract(left_side, right_side):
    return jnp.einsum("stc,stf->cf", left_side, right_side, preferred_element_type=jnp.float32)


def project_back(grad_rows, weight_full):
    return jnp.einsum("stf,cf->stc", grad_rows, weight_full, preferred_element_type=jnp.float32)


def per_device(
    hidden,
    cotangent,
    segment_ids,
    attn_gain,
    w_query,
    key_matrix,
    value_matrix,
    w_out,
    mlp_gain,
    w_gate,
    w_up,
    w_down,
):
    shards = (attn_gain, w_query, key_matrix, value_matrix, w_out, mlp_gain, w_gate, w_up, w_down)
    span_len = hidden.shape[1]
    model_width = hidden.shape[2]
    seq_count = hidden.shape[0] // MB
    head_size = key_matrix.shape[1]
    local_heads = w_query.shape[1] // head_size
    seq_len = span_len * lax.axis_size("ctx")
    score_scale = head_size ** (-0.5)
    positions_q = lax.axis_index("ctx") * span_len + jnp.arange(span_len, dtype=jnp.int32)
    positions_k = jnp.arange(seq_len, dtype=jnp.int32)
    cosine, sine_table = angles_for(positions_q, head_size)
    cos_heads = cosine[:, None, :]
    sin_heads = sine_table[:, None, :]
    causal = positions_q[:, None] >= positions_k[None, :]
    grad_list = [
        jnp.zeros((model_width,), jnp.float32),
        jnp.zeros((model_width, w_query.shape[1]), jnp.float32),
        jnp.zeros((model_width, key_matrix.shape[1]), jnp.float32),
        jnp.zeros((model_width, value_matrix.shape[1]), jnp.float32),
        jnp.zeros((w_out.shape[0], model_width), jnp.float32),
        jnp.zeros((model_width,), jnp.float32),
        jnp.zeros((model_width, w_gate.shape[1]), jnp.float32),
        jnp.zeros((model_width, w_up.shape[1]), jnp.float32),
        jnp.zeros((w_down.shape[0], model_width), jnp.float32),
    ]
    outputs = []
    input_grads = []
    for batch_index in range(MB):
        gathered = collect(shards)
        gain_one, query_w, key_w, value_w, out_w, gain_two, gate_w, up_w, down_w = gathered
        gain_one = gain_one.astype(jnp.float32)
        gain_two = gain_two.astype(jnp.float32)
        row_range = slice(batch_index * seq_count, (batch_index + 1) * seq_count)
        source = hidden[row_range].astype(jnp.float32)
        seg_local = segment_ids[row_range]
        inv_one = inv_rms(source)
        first_normalized = (source * inv_one * gain_one).astype(jnp.bfloat16)
        query_proj = jnp.dot(first_normalized, query_w, preferred_element_type=jnp.float32)
        projected_keys = jnp.dot(first_normalized, key_w, preferred_element_type=jnp.float32)
        projected_values = jnp.dot(first_normalized, value_w, preferred_element_type=jnp.float32)
        query_rows = rotary(
            query_proj.reshape(seq_count, span_len, local_heads, head_size), cos_heads, sin_heads
        ).astype(jnp.bfloat16)
        keys_local = rotary(projected_keys, cosine, sine_table).astype(jnp.bfloat16)
        values_local = projected_values.astype(jnp.bfloat16)
        keys_all, values_all, seg_all = (
            lax.all_gather(keys_local, "ctx", axis=1, tiled=True),
            lax.all_gather(values_local, "ctx", axis=1, tiled=True),
            lax.all_gather(seg_local.astype(jnp.bfloat16), "ctx", axis=1, tiled=True),
        )
        allowed = (seg_local[:, :, None] == seg_all.astype(jnp.int32)[:, None, :]) & causal[None]
        allowed = allowed[:, None]
        logits = (
            jnp.einsum("sqhd,skd->shqk", query_rows, keys_all, preferred_element_type=jnp.float32)
            * score_scale
        )
        logits = jnp.where(allowed, logits, NEG_FILL)
        row_peak = jnp.max(logits, axis=-1, keepdims=True)
        shifted = jnp.exp(logits - row_peak)
        totals = jnp.sum(shifted, axis=-1, keepdims=True)
        probs_low = (shifted / totals).astype(jnp.bfloat16)
        log_norm = row_peak + jnp.log(totals)
        heads_out = jnp.einsum(
            "shqk,skd->sqhd", probs_low, values_all, preferred_element_type=jnp.float32
        )
        heads_out = heads_out.reshape(seq_count, span_len, local_heads * head_size).astype(
            jnp.bfloat16
        )
        attn_out = lax.psum(jnp.dot(heads_out, out_w, preferred_element_type=jnp.float32), "tensor")
        residual = source + attn_out
        inv_two = inv_rms(residual)
        normed_two = (residual * inv_two * gain_two).astype(jnp.bfloat16)
        gate_pre = jnp.dot(normed_two, gate_w, preferred_element_type=jnp.float32)
        up_pre = jnp.dot(normed_two, up_w, preferred_element_type=jnp.float32)
        gate_sigmoid = jax.nn.sigmoid(gate_pre)
        silu_gate = gate_pre * gate_sigmoid
        activated = (silu_gate * up_pre).astype(jnp.bfloat16)
        mlp_out = lax.psum(
            jnp.dot(activated, down_w, preferred_element_type=jnp.float32).astype(jnp.bfloat16),
            "tensor",
        ).astype(jnp.float32)
        outputs.append((residual + mlp_out).astype(jnp.bfloat16))
        grad_top = cotangent[row_range]
        grad_list[8] = grad_list[8] + contract(activated, grad_top)
        d_act = project_back(grad_top, down_w)
        d_gate = (d_act * up_pre * gate_sigmoid * (1.0 + gate_pre * (1.0 - gate_sigmoid))).astype(
            jnp.bfloat16
        )
        d_up = (d_act * silu_gate).astype(jnp.bfloat16)
        grad_list[6] = grad_list[6] + contract(normed_two, d_gate)
        grad_list[7] = grad_list[7] + contract(normed_two, d_up)
        mlp_partial = project_back(d_gate, gate_w) + project_back(d_up, up_w)
        d_normed_two = lax.psum(mlp_partial, "tensor")
        d_norm_two, gain_term_two = norm_back(d_normed_two, residual, inv_two, gain_two)
        d_residual = grad_top.astype(jnp.float32) + d_norm_two
        d_residual_low = d_residual.astype(jnp.bfloat16)
        grad_list[5] = grad_list[5] + gain_term_two
        grad_list[4] = grad_list[4] + contract(heads_out, d_residual_low)
        d_heads = project_back(d_residual_low, out_w).astype(jnp.bfloat16)
        d_heads = d_heads.reshape(seq_count, span_len, local_heads, head_size)
        again = (
            jnp.einsum("sqhd,skd->shqk", query_rows, keys_all, preferred_element_type=jnp.float32)
            * score_scale
        )
        again = jnp.where(allowed, again, NEG_FILL)
        probs_again = jnp.exp(again - log_norm)
        probs_again_low = probs_again.astype(jnp.bfloat16)
        d_probs = jnp.einsum(
            "sqhd,skd->shqk", d_heads, values_all, preferred_element_type=jnp.float32
        )
        row_delta = jnp.sum(probs_again * d_probs, axis=-1, keepdims=True)
        d_scores = (probs_again * (d_probs - row_delta)).astype(jnp.bfloat16)
        d_query = (
            jnp.einsum("shqk,skd->sqhd", d_scores, keys_all, preferred_element_type=jnp.float32)
            * score_scale
        )
        key_terms = (
            jnp.einsum("shqk,sqhd->ksd", d_scores, query_rows, preferred_element_type=jnp.float32)
            * score_scale
        )
        value_terms = jnp.einsum(
            "shqk,sqhd->ksd", probs_again_low, d_heads, preferred_element_type=jnp.float32
        )
        kv_terms = jnp.stack([key_terms, value_terms], axis=1).reshape(
            seq_len, 2 * seq_count * head_size
        )
        kv_local = lax.psum_scatter(kv_terms, "ctx", scatter_dimension=0, tiled=True).reshape(
            span_len, 2, seq_count, head_size
        )
        d_key = jnp.transpose(kv_local[:, 0], (1, 0, 2))
        d_value = jnp.transpose(kv_local[:, 1], (1, 0, 2))
        d_query_proj = rotary(d_query, cos_heads, -sin_heads).astype(jnp.bfloat16)
        d_query_proj = d_query_proj.reshape(seq_count, span_len, local_heads * head_size)
        d_key_proj = rotary(d_key, cosine, -sine_table).astype(jnp.bfloat16)
        d_value_proj = d_value.astype(jnp.bfloat16)
        grad_list[1] = grad_list[1] + contract(first_normalized, d_query_proj)
        grad_list[2] = grad_list[2] + contract(first_normalized, d_key_proj)
        grad_list[3] = grad_list[3] + contract(first_normalized, d_value_proj)
        attn_partial = (
            project_back(d_query_proj, query_w)
            + project_back(d_key_proj, key_w)
            + project_back(d_value_proj, value_w)
        )
        d_normed_one = lax.psum(attn_partial, "tensor")
        d_norm_one, gain_term_one = norm_back(d_normed_one, source, inv_one, gain_one)
        grad_list[0] = grad_list[0] + gain_term_one
        input_grads.append(d_residual + d_norm_one)
    input_grad_rows = jnp.concatenate(input_grads, axis=0)
    summed = (
        lax.psum_scatter(grad_list[0], ("dp", "ctx"), scatter_dimension=0, tiled=True),
        lax.psum_scatter(grad_list[1], ("dp", "ctx"), scatter_dimension=0, tiled=True),
        lax.psum_scatter(grad_list[2], ("dp", "ctx"), scatter_dimension=0, tiled=True),
        lax.psum_scatter(grad_list[3], ("dp", "ctx"), scatter_dimension=0, tiled=True),
        lax.psum_scatter(grad_list[4], ("dp", "ctx"), scatter_dimension=1, tiled=True),
        lax.psum_scatter(grad_list[5], ("dp", "ctx"), scatter_dimension=0, tiled=True),
        lax.psum_scatter(grad_list[6], ("dp", "ctx"), scatter_dimension=0, tiled=True),
        lax.psum_scatter(grad_list[7], ("dp", "ctx"), scatter_dimension=0, tiled=True),
        lax.psum_scatter(grad_list[8], ("dp", "ctx"), scatter_dimension=1, tiled=True),
    )
    return (
        jnp.concatenate(outputs, axis=0),
        input_grad_rows,
        summed[0],
        summed[1],
        summed[2],
        summed[3],
        summed[4],
        summed[5],
        summed[6],
        summed[7],
        summed[8],
    )


def solution(mesh):
    in_specs = (
        P("dp", "ctx", None),
        P("dp", "ctx", None),
        P("dp", "ctx"),
        P(("dp", "ctx")),
        P(("dp", "ctx"), "tensor"),
        P(("dp", "ctx"), "tensor"),
        P(("dp", "ctx"), "tensor"),
        P("tensor", ("dp", "ctx")),
        P(("dp", "ctx")),
        P(("dp", "ctx"), "tensor"),
        P(("dp", "ctx"), "tensor"),
        P("tensor", ("dp", "ctx")),
    )
    out_specs = (
        P("dp", "ctx", None),
        P("dp", "ctx", None),
        P(("dp", "ctx")),
        P(("dp", "ctx"), "tensor"),
        P(("dp", "ctx"), "tensor"),
        P(("dp", "ctx"), "tensor"),
        P("tensor", ("dp", "ctx")),
        P(("dp", "ctx")),
        P(("dp", "ctx"), "tensor"),
        P(("dp", "ctx"), "tensor"),
        P("tensor", ("dp", "ctx")),
    )
    return jax.shard_map(
        per_device, mesh=mesh, in_specs=in_specs, out_specs=out_specs, check_vma=False
    )
```

profile of v0, /device:TPU:0, one launch (start us, length us, event | category | flops | bytes accessed | tf_op | source)
XLA Modules:
  0.0 1380.9 jit_solution(2608815866896692798)
XLA Ops:
  11.5 10.4 all-gather.2
  22.0 9.8 all_gather.58
  32.9 9.8 all_gather.55
  43.7 5.1 all_gather.57
  48.7 5.1 all_gather.67
  54.9 5.4 all_gather.68
  60.3 6.0 all_gather.59
  66.3 5.4 all-gather
  71.7 6.1 all-gather.1
  78.5 3.9 copy.47
  82.4 2.6 convolution_bitcast_fusion.2
  95.2 3.8 convolution_bitcast_fusion.1
  99.0 2.0 convolution_bitcast_fusion
  102.9 9.4 all-gather.3
  112.3 144.4 %all-reduce.16.cloned.1.call-done = (f32[1,256,2048]{2,1,0:T(8,128)}, f32[1,256,2048]{2,1,0:T(8,128)}) async-done(((f32[1,256,2048]{2,1,0:T(8,128)}, f32[1,256,2048]{2,1,0:T(8,128)}), (f32[1,256,2048]{2,1,0:T(8,128)}, f32[1,256,2048]{2,1,0:T(8,128)})) %all-reduce.16.cloned.1.call-update) | async-done | bytes 4194320 | tf_op jit(solution)/shard_map/psum | solution.py:148
  256.7 2.8 multiply_reduce_fusion.5
  262.9 37.8 %all-gather.16.cloned.1.call-done = bf16[2048,1408]{1,0:T(8,128)(2,1)} async-done(((bf16[256,1408]{1,0:T(8,128)(2,1)}), bf16[2048,1408]{1,0:T(8,128)(2,1)}) %all-gather.16.cloned.1.call-update) | async-done | bytes 5767184 | tf_op jit(solution)/shard_map/all_gather | solution.py:53
  300.6 5.9 fusion.193
  306.5 39.1 %all-gather.14.cloned.1.call-done = bf16[2048,1408]{1,0:T(8,128)(2,1)} async-done(((bf16[256,1408]{1,0:T(8,128)(2,1)}), bf16[2048,1408]{1,0:T(8,128)(2,1)}) %all-gather.14.cloned.1.call-update) | async-done | bytes 5767184 | tf_op jit(solution)/shard_map/all_gather | solution.py:52
  345.6 6.0 fusion.192
  351.6 2.9 fusion.195
  354.5 2.9 fusion.194
  357.5 34.2 %all-gather.18.cloned.1.call-done = bf16[1408,2048]{1,0:T(8,128)(2,1)} async-done(((bf16[1408,256]{1,0:T(8,128)(2,1)}), bf16[1408,2048]{1,0:T(8,128)(2,1)}) %all-gather.18.cloned.1.call-update) | async-done | bytes 5767184 | tf_op jit(solution)/shard_map/all_gather | solution.py:54
  391.6 7.1 multiply_convert_fusion.2
  399.6 4.6 fusion.198
  404.5 3.7 multiply_convert_fusion.4
  410.1 3.1 fusion.35
  413.3 3.1 fusion.34
  416.5 5.7 fusion.36
  422.2 5.7 fusion.37
  429.2 142.4 %all-reduce.14.cloned.1.call-done = (f32[1,256,2048]{2,1,0:T(8,128)}, f32[1,256,2048]{2,1,0:T(8,128)}) async-done(((f32[1,256,2048]{2,1,0:T(8,128)}, f32[1,256,2048]{2,1,0:T(8,128)}), (f32[1,256,2048]{2,1,0:T(8,128)}, f32[1,256,2048]{2,1,0:T(8,128)})) %all-reduce.14.cloned.1.call-update) | async-done | bytes 4194320 | tf_op jit(solution)/shard_map/psum | solution.py:172
  571.6 5.0 multiply_reduce_fusion.1
  576.6 83.1 %all-reduce.18.cloned.1.call-done = (bf16[1,256,2048]{2,1,0:T(8,128)(2,1)}, bf16[1,256,2048]{2,1,0:T(8,128)(2,1)}) async-done(((bf16[1,256,2048]{2,1,0:T(8,128)(2,1)}, bf16[1,256,2048]{2,1,0:T(8,128)(2,1)}), (bf16[1,256,2048]{2,1,0:T(8,128)(2,1)}, bf16[1,256,2048]{2,1,0:T(8,128)(2,1)})) %all-reduce.18.cloned.1.call-update) | async-done | bytes 2097168 | tf_op jit(solution)/shard_map/psum | solution.py:157
  659.8 7.3 multiply_add_fusion.1
  671.0 5.5 fusion.65
  676.6 8.8 fusion
  688.0 5.7 fusion.62
  693.6 8.9 fusion.3
  707.5 7.0 fusion.16
  722.1 2.1 fusion.199
  724.2 2.1 fusion.197
  728.9 23.7 %reduce-scatter.10.cloned.1.call-done = f32[256,128]{0,1:T(8,128)} async-done(((f32[1024,128]{0,1:T(8,128)}), f32[256,128]{0,1:T(8,128)}) %reduce-scatter.10.cloned.1.call-update) | async-done | bytes 131088 | tf_op jit(solution)/shard_map/reduce_scatter | solution.py:206
  754.4 2.1 convolution_add_fusion.6
  766.5 2.8 fusion.79
  769.3 2.7 convolution_add_fusion.3
  773.9 2.9 convolution_add_fusion.4
  777.1 3.3 fusion.201
  780.4 6.1 convolution_add_fusion.1
  786.7 3.3 fusion.200
  790.0 6.1 convolution_add_fusion.2
  797.2 3.1 fusion.82
  800.3 5.9 convolution_add_fusion
  808.1 2.7 pad_maximum_fusion.1
  810.9 105.5 %all-reduce.12.cloned.1.call-done = (f32[1,256,2048]{2,1,0:T(8,128)}, f32[1,256,2048]{2,1,0:T(8,128)}) async-done(((f32[1,256,2048]{2,1,0:T(8,128)}, f32[1,256,2048]{2,1,0:T(8,128)}), (f32[1,256,2048]{2,1,0:T(8,128)}, f32[1,256,2048]{2,1,0:T(8,128)})) %all-reduce.12.cloned.1.call-update) | async-done | bytes 4194320 | tf_op jit(solution)/shard_map/psum | solution.py:223
  916.4 3.3 fusion.43
  919.7 23.9 %all-reduce.2 = (f32[2048]{0:T(1024)S(1)}, f32[2048]{0:T(1024)S(1)}) all-reduce(f32[2048]{0:T(1024)S(1)} %add.260, f32[2048]{0:T(1024)S(1)} %add.265), channel_id=6, replica_groups=mesh['dp'=2,'ctx'=4,'tensor'=4] {'dp','ctx'}, use_global_device_ids=true, to_apply=%region_26.27.clone | all-reduce | flops 4096 | bytes 32768
  944.9 4.5 fusion.42
  949.4 2.5 pad_maximum_fusion
  953.0 37.8 %reduce-scatter.18.cloned.1.call-done = f32[256,64]{0,1:T(8,128)} async-done(((f32[2048,64]{0,1:T(8,128)}), f32[256,64]{0,1:T(8,128)}) %reduce-scatter.18.cloned.1.call-update) | async-done | bytes 65552 | tf_op jit(solution)/shard_map/reduce_scatter | solution.py:232
  990.8 54.9 %reduce-scatter.20.cloned.1.call-done = f32[512,256]{1,0:T(8,128)} async-done(((f32[512,2048]{1,0:T(8,128)}), f32[512,256]{1,0:T(8,128)}) %reduce-scatter.20.cloned.1.call-update) | async-done | bytes 524304 | tf_op jit(solution)/shard_map/reduce_scatter | solution.py:233
  1045.7 55.0 %reduce-scatter.14.cloned.1.call-done = f32[256,512]{1,0:T(8,128)} async-done(((f32[2048,512]{1,0:T(8,128)}), f32[256,512]{1,0:T(8,128)}) %reduce-scatter.14.cloned.1.call-update) | async-done | bytes 524304 | tf_op jit(solution)/shard_map/reduce_scatter | solution.py:230
  1100.7 91.1 %reduce-scatter.24.cloned.1.call-done = f32[256,1408]{1,0:T(8,128)} async-done(((f32[2048,1408]{1,0:T(8,128)}), f32[256,1408]{1,0:T(8,128)}) %reduce-scatter.24.cloned.1.call-update) | async-done | bytes 1441808 | tf_op jit(solution)/shard_map/reduce_scatter | solution.py:236
  1191.8 91.1 %reduce-scatter.22.cloned.1.call-done = f32[256,1408]{1,0:T(8,128)} async-done(((f32[2048,1408]{1,0:T(8,128)}), f32[256,1408]{1,0:T(8,128)}) %reduce-scatter.22.cloned.1.call-update) | async-done | bytes 1441808 | tf_op jit(solution)/shard_map/reduce_scatter | solution.py:235
  1282.9 90.8 %reduce-scatter.26.cloned.1.call-done = f32[1408,256]{1,0:T(8,128)} async-done(((f32[1408,2048]{1,0:T(8,128)}), f32[1408,256]{1,0:T(8,128)}) %reduce-scatter.26.cloned.1.call-update) | async-done | bytes 1441808 | tf_op jit(solution)/shard_map/reduce_scatter | solution.py:237
  (322 shorter events, 67.3 us)
Async XLA Ops:
  7.2 24.6 %copy-start.2 = (bf16[2,256,2048]{2,1,0:T(8,128)(2,1)S(1)}, bf16[2,256,2048]{2,1,0:T(8,128)(2,1)}, u32[]{:S(2)}) copy-start(bf16[2,256,2048]{2,1,0:T(8,128)(2,1)} %param.12) | copy-start | bytes 6291460
  7.2 14.8 %copy-start.77 = (bf16[256,64]{0,1:T(8,128)(2,1)S(1)}, bf16[256,64]{0,1:T(8,128)(2,1)}, u32[]{:S(2)}) copy-start(bf16[256,64]{0,1:T(8,128)(2,1)} %param.17) | copy-start | bytes 98308
  7.2 71.3 %all-gather.10.cloned.1.call-start = ((), (), s32[]{:S(2)}) async-start(), calls=%async_computation.9 | async-start | bytes 2359296 | tf_op jit(solution)/shard_map/all_gather | solution.py:47
  7.9 87.2 %all-gather.12.cloned.1.call-start = ((), (), s32[]{:S(2)}) async-start(), calls=%async_computation.10 | async-start | bytes 2359296 | tf_op jit(solution)/shard_map/all_gather | solution.py:50
  8.7 248.0 %all-reduce.16.cloned.1.call-start = ((), (), s32[]{:S(2)}) async-start(), calls=%async_computation.25 | async-start | bytes 8388608 | tf_op jit(solution)/shard_map/psum | solution.py:148
  8.7 45.9 %copy-start.85 = (f32[32]{0:T(128)}, f32[32]{0:T(128)S(1)}, u32[]{:S(2)}) copy-start(f32[32]{0:T(128)S(1)} %multiply_power_fusion) | copy-start | bytes 388
  8.8 45.9 %copy-start.83 = (f32[256]{0:T(256)}, f32[256]{0:T(256)S(1)}, u32[]{:S(2)}) copy-start(f32[256]{0:T(256)S(1)} %fusion.169) | copy-start | bytes 3076
  11.5 73.5 %copy-start.79 = (f32[256]{0:T(256)}, f32[256]{0:T(256)S(1)}, u32[]{:S(2)}) copy-start(f32[256]{0:T(256)S(1)} %add_rsqrt_fusion.3) | copy-start | bytes 3076
  11.5 70.9 %copy-start.81 = (f32[256]{0:T(256)}, f32[256]{0:T(256)S(1)}, u32[]{:S(2)}) copy-start(f32[256]{0:T(256)S(1)} %add_rsqrt_fusion.1) | copy-start | bytes 3076
  66.3 19.8 %copy-start.29 = (bf16[1,1024,64]{1,2,0:T(8,128)(2,1)}, bf16[1,1024,64]{1,2,0:T(8,128)(2,1)S(1)}, u32[]{:S(2)}) copy-start(bf16[1,1024,64]{1,2,0:T(8,128)(2,1)S(1)} %all_gather.59) | copy-start | bytes 393220
  71.7 19.5 %copy-start.52 = (bf16[1024,64]{0,1:T(8,128)(2,1)}, bf16[1024,64]{0,1:T(8,128)(2,1)S(1)}, u32[]{:S(2)}) copy-start(bf16[1024,64]{0,1:T(8,128)(2,1)S(1)} %all-gather) | copy-start | bytes 393220
  87.5 3.7 copy-start
  87.5 3.7 copy-start.64
  88.9 4.7 copy-start.1
  95.1 3.8 copy-start.43
  95.2 3.8 copy-start.7
  101.1 199.6 %all-gather.16.cloned.1.call-start = ((), (), s32[]{:S(2)}) async-start(), calls=%async_computation.12 | async-start | bytes 6488064 | tf_op jit(solution)/shard_map/all_gather | solution.py:53
  101.6 243.9 %all-gather.14.cloned.1.call-start = ((), (), s32[]{:S(2)}) async-start(), calls=%async_computation.11 | async-start | bytes 6488064 | tf_op jit(solution)/shard_map/all_gather | solution.py:52
  102.2 289.4 %all-gather.18.cloned.1.call-start = ((), (), s32[]{:S(2)}) async-start(), calls=%async_computation.13 | async-start | bytes 6488064 | tf_op jit(solution)/shard_map/all_gather | solution.py:54
  102.8 468.8 %all-reduce.14.cloned.1.call-start = ((), (), s32[]{:S(2)}) async-start(), calls=%async_computation.24 | async-start | bytes 8388608 | tf_op jit(solution)/shard_map/psum | solution.py:172
  345.6 6.0 copy-start.89
  345.6 8.9 slice-start.6
  391.6 12.6 copy-start.92
  391.6 12.6 copy-start.93
  398.7 14.6 %copy-start.50 = (bf16[256,1408]{1,0:T(8,128)(2,1)}, bf16[256,1408]{1,0:T(8,128)(2,1)S(1)}, u32[]{:S(2)}) copy-start(bf16[256,1408]{1,0:T(8,128)(2,1)S(1)} %get-tuple-element.40) | copy-start | bytes 2162692
  399.6 4.7 copy-start.14
  399.6 5.0 copy-start.88
  399.6 8.7 slice-start.8
  399.6 10.5 slice-start.4
  404.5 3.7 slice-start.9
  404.5 5.6 slice-start.5
  416.5 243.3 %all-reduce.18.cloned.1.call-start = ((), (), s32[]{:S(2)}) async-start(), calls=%async_computation.26 | async-start | bytes 4194304 | tf_op jit(solution)/shard_map/psum | solution.py:157
  416.5 5.7 copy-start.18
  427.9 300.2 %reduce-scatter.12.cloned.1.call-start = ((), (), s32[]{:S(2)}) async-start(), calls=%async_computation.15 | async-start | bytes 655360 | tf_op jit(solution)/shard_map/reduce_scatter | solution.py:206
  659.8 8.7 copy-start.8
  671.0 5.6 copy-start.55
  671.0 5.5 copy-start.58
  676.6 8.8 copy-start.9
  676.6 8.8 copy-start.10
  687.9 5.7 copy-start.53
  688.0 14.6 %slice-start = ((s8[8388608]{0:T(1024)(128)(4,1)}), s8[4194304]{0:T(1024)(128)(4,1)S(1)}, s32[]{:S(2)}) async-start(s8[8388608]{0:T(1024)(128)(4,1)} %bitcast.333), calls=%async_computation.27 | async-start | bytes 8388608
  688.0 14.6 %slice-start.2 = ((s8[8388608]{0:T(1024)(128)(4,1)}), s8[4194304]{0:T(1024)(128)(4,1)S(1)}, s32[]{:S(2)}) async-start(s8[8388608]{0:T(1024)(128)(4,1)} %bitcast.335), calls=%async_computation.29 | async-start | bytes 8388608
  693.6 9.0 slice-start.1
  693.6 9.0 slice-start.3
  693.6 9.0 copy-start.59
  693.6 9.0 copy-start.74
  707.2 45.4 %reduce-scatter.10.cloned.1.call-start = ((), (), s32[]{:S(2)}) async-start(), calls=%async_computation.14 | async-start | bytes 655360 | tf_op jit(solution)/shard_map/reduce_scatter | solution.py:206
  707.5 7.0 copy-start.32
  707.5 7.0 copy-start.34
  720.1 196.2 %all-reduce.12.cloned.1.call-start = ((), (), s32[]{:S(2)}) async-start(), calls=%async_computation.23 | async-start | bytes 8388608 | tf_op jit(solution)/shard_map/psum | solution.py:223
  724.2 29.3 %copy-start.84 = (f32[256]{0:T(256)S(1)}, f32[256]{0:T(256)}, u32[]{:S(2)}) copy-start(f32[256]{0:T(256)} %copy-done.83) | copy-start | bytes 3076
  724.2 29.3 %copy-start.86 = (f32[32]{0:T(128)S(1)}, f32[32]{0:T(128)}, u32[]{:S(2)}) copy-start(f32[32]{0:T(128)} %copy-done.85) | copy-start | bytes 388
  724.2 30.2 %copy-start.21 = (bf16[2048,64]{0,1:T(8,128)(2,1)S(1)}, bf16[2048,64]{0,1:T(8,128)(2,1)}, u32[]{:S(2)}) copy-start(bf16[2048,64]{0,1:T(8,128)(2,1)} %copy-done.20) | copy-start | bytes 786436
  753.8 4.5 copy-start.70
  753.8 4.5 copy-start.72
  761.2 191.8 %reduce-scatter.16.cloned.1.call-start = ((), (), s32[]{:S(2)}) async-start(), calls=%async_computation.17 | async-start | bytes 589824 | tf_op jit(solution)/shard_map/reduce_scatter | solution.py:231
  763.7 227.1 %reduce-scatter.18.cloned.1.call-start = ((), (), s32[]{:S(2)}) async-start(), calls=%async_computation.18 | async-start | bytes 589824 | tf_op jit(solution)/shard_map/reduce_scatter | solution.py:232
  766.4 279.3 %reduce-scatter.20.cloned.1.call-start = ((), (), s32[]{:S(2)}) async-start(), calls=%async_computation.19 | async-start | bytes 4718592 | tf_op jit(solution)/shard_map/reduce_scatter | solution.py:233
  772.0 328.7 %reduce-scatter.14.cloned.1.call-start = ((), (), s32[]{:S(2)}) async-start(), calls=%async_computation.16 | async-start | bytes 4718592 | tf_op jit(solution)/shard_map/reduce_scatter | solution.py:230
  776.8 415.0 %reduce-scatter.24.cloned.1.call-start = ((), (), s32[]{:S(2)}) async-start(), calls=%async_computation.21 | async-start | bytes 12976128 | tf_op jit(solution)/shard_map/reduce_scatter | solution.py:236
  777.1 3.3 copy-start.51
  786.6 496.3 %reduce-scatter.22.cloned.1.call-start = ((), (), s32[]{:S(2)}) async-start(), calls=%async_computation.20 | async-start | bytes 12976128 | tf_op jit(solution)/shard_map/reduce_scatter | solution.py:235
  796.1 4.2 copy-start.19
  796.1 577.5 %reduce-scatter.26.cloned.1.call-start = ((), (), s32[]{:S(2)}) async-start(), calls=%async_computation.22 | async-start | bytes 12976128 | tf_op jit(solution)/shard_map/reduce_scatter | solution.py:237
  (58 other events, 94.0 us)
Sparse Core Ops, SparseCore 0:
  9.9 31.1 all-gather.9
  43.0 28.4 all-gather.11
  101.2 155.4 all-reduce.15
  258.4 42.1 all-gather.15
  302.4 43.1 all-gather.13
  347.3 44.2 all-gather.17
  416.6 154.9 all-reduce.13
  574.6 85.1 all-reduce.17
  707.4 20.6 reduce-scatter.11
  731.0 21.6 reduce-scatter.9
  761.3 155.0 all-reduce.11
  919.9 33.0 reduce-scatter.15
  956.6 34.1 reduce-scatter.17
  994.6 51.0 reduce-scatter.19
  1049.5 51.1 reduce-scatter.13
  1104.6 87.1 reduce-scatter.23
  1195.7 87.1 reduce-scatter.21
  1286.8 86.8 reduce-scatter.25
where the time goes:
time: 1390 us; the launch traced here: 1380 us
  waiting for transfers between devices  1040 us (75%)
  matrix products  159 us (11%)
  blocking collectives  96.4 us (7%)
  other arithmetic  48.5 us (3%)
  local copies, waits for them, and re-layouts  21.8 us (2%)
  between operations  16.7 us (1%)
    psum x1, waiting for transfers between devices, per_device(): lax.psum(jnp.dot(heads_out, out_w, preferred_element_type=jnp.float32), '...  144 us
    psum x1, waiting for transfers between devices, per_device(): d_normed_two = lax.psum(mlp_partial, 'tensor')  142 us
    psum x1, waiting for transfers between devices, per_device(): d_normed_one = lax.psum(attn_partial, 'tensor')  106 us
    reduce_scatter x1, waiting for transfers between devices, per_device(): lax.psum_scatter(grad_list[7], ('dp', 'ctx'), scatter_dimension=0, tiled=...  91.1 us
    reduce_scatter x1, waiting for transfers between devices, per_device(): lax.psum_scatter(grad_list[6], ('dp', 'ctx'), scatter_dimension=0, tiled=...  91.1 us
    reduce_scatter x1, waiting for transfers between devices, per_device(): lax.psum_scatter(grad_list[8], ('dp', 'ctx'), scatter_dimension=1, tiled=...  90.8 us
    psum x1, waiting for transfers between devices, per_device(): lax.psum(jnp.dot(activated, down_w, preferred_element_type=jnp.float32).a...  83.1 us
    reduce_scatter x1, waiting for transfers between devices, per_device(): lax.psum_scatter(grad_list[1], ('dp', 'ctx'), scatter_dimension=0, tiled=...  55 us
  transfers between devices with their start and end apart: 18, of which 16 were waited for; matrix products, arithmetic and copies ran while one was open for 10% of the time, Pallas kernels for 0%

commit v1 on v0

--- a/solution.py
+++ b/solution.py
@@ -2,6 +2,7 @@
 import jax.numpy as jnp
 from jax import lax
 from jax.sharding import PartitionSpec as P
+from jax.lax import axis_size, ppermute
 
 MB = 2
 EPSILON = 1e-05
@@ -169,7 +170,11 @@
         grad_list[6] = grad_list[6] + contract(normed_two, d_gate)
         grad_list[7] = grad_list[7] + contract(normed_two, d_up)
         mlp_partial = project_back(d_gate, gate_w) + project_back(d_up, up_w)
-        d_normed_two = lax.psum(mlp_partial, "tensor")
+        n_blocks = axis_size("tensor")
+        d_normed_two = mlp_partial
+        for j0 in [[(p, p ^ i) for p in range(n_blocks)] for i in (1, 2, 4, 8, 16) if i < n_blocks]:
+            piece_now = ppermute(d_normed_two, axis_name="tensor", perm=j0)
+            d_normed_two = d_normed_two + piece_now
         d_norm_two, gain_term_two = norm_back(d_normed_two, residual, inv_two, gain_two)
         d_residual = grad_top.astype(jnp.float32) + d_norm_two
         d_residual_low = d_residual.astype(jnp.bfloat16)

time: 1390 us -> 1500 us (1.079)
  waiting for transfers between devices: 1040 us -> 1150 us
  matrix products: 159 us -> 143 us
    ppermute x0 -> x4, waiting for transfers between devices: none -> 333 us  [per_device(): piece_now = ppermute(d_normed_two, axis_name='tensor', perm=j0)]
    psum x1 -> x0, waiting for transfers between devices: 142 us -> none  [per_device(): d_normed_two = lax.psum(mlp_partial, 'tensor')]
    psum x1, waiting for transfers between devices: 83.1 us -> 0.01 us  [per_device(): lax.psum(jnp.dot(activated, down_w, preferred_element_type=jnp.float32).a...]
  transfers between devices with their start and end apart: 18 -> 21, of which waited for: 16 -> 18; matrix products, arithmetic and copies ran while one was open for 10% -> 8% of each run, Pallas kernels for 0% -> 0%
where the time goes in v1:
time: 1500 us
  waiting for transfers between devices  1150 us (77%)
  matrix products  143 us (10%)
  blocking collectives  96.6 us (6%)
  other arithmetic  58.1 us (4%)
  local copies, waits for them, and re-layouts  21 us (1%)
  between operations  16.2 us (1%)
    ppermute x4, waiting for transfers between devices, per_device(): piece_now = ppermute(d_normed_two, axis_name='tensor', perm=j0)  333 us
    psum x1, waiting for transfers between devices, per_device(): lax.psum(jnp.dot(heads_out, out_w, preferred_element_type=jnp.float32), '...  144 us
    psum x1, waiting for transfers between devices, per_device(): d_normed_one = lax.psum(attn_partial, 'tensor')  106 us
    reduce_scatter x1, waiting for transfers between devices, per_device(): lax.psum_scatter(grad_list[7], ('dp', 'ctx'), scatter_dimension=0, tiled=...  91.1 us
    reduce_scatter x1, waiting for transfers between devices, per_device(): lax.psum_scatter(grad_list[6], ('dp', 'ctx'), scatter_dimension=0, tiled=...  91.1 us
    reduce_scatter x1, waiting for transfers between devices, per_device(): lax.psum_scatter(grad_list[8], ('dp', 'ctx'), scatter_dimension=1, tiled=...  90.8 us
    reduce_scatter x1, waiting for transfers between devices, per_device(): lax.psum_scatter(grad_list[1], ('dp', 'ctx'), scatter_dimension=0, tiled=...  55.1 us
    reduce_scatter x1, waiting for transfers between devices, per_device(): lax.psum_scatter(grad_list[4], ('dp', 'ctx'), scatter_dimension=1, tiled=...  54.9 us
  transfers between devices with their start and end apart: 21, of which 18 were waited for; matrix products, arithmetic and copies ran while one was open for 8% of the time, Pallas kernels for 0%

profile of v1, /device:TPU:0, one launch (start us, length us, event | category | flops | bytes accessed | tf_op | source)
XLA Modules:
  0.0 1496.5 jit_solution(17346873056342966282)
XLA Ops:
  9.5 10.4 all-gather.2
  19.9 2.1 fusion.44
  22.0 9.8 all_gather.58
  32.9 9.8 all_gather.55
  44.8 5.4 all_gather.68
  50.2 5.1 all_gather.57
  55.3 5.1 all_gather.67
  60.3 6.1 all-gather.1
  66.4 5.5 all_gather.59
  71.9 6.3 all-gather
  78.9 3.9 copy.47
  82.9 2.6 convolution_bitcast_fusion.3
  95.6 3.8 convolution_bitcast_fusion
  103.3 9.3 all-gather.3
  112.6 144.4 %all-reduce.12.cloned.1.call-done = (f32[1,256,2048]{2,1,0:T(8,128)}, f32[1,256,2048]{2,1,0:T(8,128)}) async-done(((f32[1,256,2048]{2,1,0:T(8,128)}, f32[1,256,2048]{2,1,0:T(8,128)}), (f32[1,256,2048]{2,1,0:T(8,128)}, f32[1,256,2048]{2,1,0:T(8,128)})) %all-reduce.12.cloned.1.call-update) | async-done | bytes 4194320 | tf_op jit(solution)/shard_map/psum | solution.py:149
  257.1 4.1 multiply_reduce_fusion.5
  262.7 38.3 %all-gather.14.cloned.1.call-done = bf16[2048,1408]{1,0:T(8,128)(2,1)} async-done(((bf16[256,1408]{1,0:T(8,128)(2,1)}), bf16[2048,1408]{1,0:T(8,128)(2,1)}) %all-gather.14.cloned.1.call-update) | async-done | bytes 5767184 | tf_op jit(solution)/shard_map/all_gather | solution.py:53
  301.0 5.5 fusion.192
  306.5 39.4 %all-gather.16.cloned.1.call-done = bf16[2048,1408]{1,0:T(8,128)(2,1)} async-done(((bf16[256,1408]{1,0:T(8,128)(2,1)}), bf16[2048,1408]{1,0:T(8,128)(2,1)}) %all-gather.16.cloned.1.call-update) | async-done | bytes 5767184 | tf_op jit(solution)/shard_map/all_gather | solution.py:54
  345.9 5.5 fusion.193
  351.5 40.5 %all-gather.18.cloned.1.call-done = bf16[1408,2048]{1,0:T(8,128)(2,1)} async-done(((bf16[1408,256]{1,0:T(8,128)(2,1)}), bf16[1408,2048]{1,0:T(8,128)(2,1)}) %all-gather.18.cloned.1.call-update) | async-done | bytes 5767184 | tf_op jit(solution)/shard_map/all_gather | solution.py:55
  392.0 6.2 multiply_convert_fusion.4
  405.0 46.3 %collective-permute-done = f32[1,256,2048]{2,1,0:T(8,128)S(1)} collective-permute-done((f32[1,256,2048]{2,1,0:T(8,128)S(1)}, f32[1,256,2048]{2,1,0:T(8,128)S(1)}, u32[]{:S(2)}, u32[]{:S(2)}) %collective-permute-start) | collective-permute-done | bytes 2097184 | tf_op jit(solution)/shard_map/ppermute | solution.py:176
  451.6 2.5 collective-permute-start.1
  455.9 88.5 %collective-permute-done.1 = f32[1,256,2048]{2,1,0:T(8,128)S(1)} collective-permute-done((f32[1,256,2048]{2,1,0:T(8,128)S(1)}, f32[1,256,2048]{2,1,0:T(8,128)S(1)}, u32[]{:S(2)}, u32[]{:S(2)}) %collective-permute-start.1) | collective-permute-done | bytes 2097184 | tf_op jit(solution)/shard_map/ppermute | solution.py:176
  547.8 2.4 multiply_convert_fusion.2
  554.5 46.1 %collective-permute-done.2 = f32[1,256,2048]{2,1,0:T(8,128)S(1)} collective-permute-done((f32[1,256,2048]{2,1,0:T(8,128)S(1)}, f32[1,256,2048]{2,1,0:T(8,128)S(1)}, u32[]{:S(2)}, u32[]{:S(2)}) %collective-permute-start.2) | collective-permute-done | bytes 2097184 | tf_op jit(solution)/shard_map/ppermute | solution.py:176
  602.3 3.1 collective-permute-start.3
  605.4 2.8 fusion.36
  608.2 2.9 fusion.37
  612.1 151.6 %collective-permute-done.3 = f32[1,256,2048]{2,1,0:T(8,128)} collective-permute-done((f32[1,256,2048]{2,1,0:T(8,128)}, f32[1,256,2048]{2,1,0:T(8,128)}, u32[]{:S(2)}, u32[]{:S(2)}) %collective-permute-start.3) | collective-permute-done | bytes 2097184 | tf_op jit(solution)/shard_map/ppermute | solution.py:176
  763.7 4.1 multiply_reduce_fusion
  767.9 9.1 multiply_add_fusion.1
  780.8 8.7 fusion.3
  789.6 5.6 fusion.62
  797.7 8.9 fusion
  806.6 5.5 fusion.65
  812.2 6.8 fusion.16
  822.1 7.0 fusion.17
  838.9 2.1 fusion.196
  841.0 2.8 reduce-scatter.10.cloned.1.call-done
  844.7 23.9 %reduce-scatter.12.cloned.1.call-done = f32[256,128]{0,1:T(8,128)} async-done(((f32[1024,128]{0,1:T(8,128)}), f32[256,128]{0,1:T(8,128)}) %reduce-scatter.12.cloned.1.call-update) | async-done | bytes 131088 | tf_op jit(solution)/shard_map/reduce_scatter | solution.py:211
  870.3 2.1 convolution_add_fusion.6
  883.4 2.9 convolution_add_fusion.4
  887.2 2.5 fusion.79
  889.7 2.7 convolution_add_fusion.3
  892.7 3.4 fusion.199
  896.1 6.1 convolution_add_fusion.2
  902.3 3.3 fusion.200
  905.6 6.1 convolution_add_fusion.1
  912.9 3.1 fusion.82
  916.0 5.9 convolution_add_fusion
  923.8 2.7 pad_maximum_fusion.1
  926.6 105.7 %all-reduce.10.cloned.1.call-done = (f32[1,256,2048]{2,1,0:T(8,128)}, f32[1,256,2048]{2,1,0:T(8,128)}) async-done(((f32[1,256,2048]{2,1,0:T(8,128)}, f32[1,256,2048]{2,1,0:T(8,128)}), (f32[1,256,2048]{2,1,0:T(8,128)}, f32[1,256,2048]{2,1,0:T(8,128)})) %all-reduce.10.cloned.1.call-update) | async-done | bytes 4194320 | tf_op jit(solution)/shard_map/psum | solution.py:228
  1032.3 3.3 fusion.43
  1035.6 23.9 %all-reduce.2 = (f32[2048]{0:T(1024)S(1)}, f32[2048]{0:T(1024)S(1)}) all-reduce(f32[2048]{0:T(1024)S(1)} %add.272, f32[2048]{0:T(1024)S(1)} %add.277), channel_id=6, replica_groups=mesh['dp'=2,'ctx'=4,'tensor'=4] {'dp','ctx'}, use_global_device_ids=true, to_apply=%region_24.25.clone | all-reduce | flops 4096 | bytes 32768
  1060.8 4.5 fusion.42
  1065.4 2.5 pad_maximum_fusion
  1069.1 37.7 %reduce-scatter.18.cloned.1.call-done = f32[256,64]{0,1:T(8,128)} async-done(((f32[2048,64]{0,1:T(8,128)}), f32[256,64]{0,1:T(8,128)}) %reduce-scatter.18.cloned.1.call-update) | async-done | bytes 65552 | tf_op jit(solution)/shard_map/reduce_scatter | solution.py:237
  1106.7 55.1 %reduce-scatter.14.cloned.1.call-done = f32[256,512]{1,0:T(8,128)} async-done(((f32[2048,512]{1,0:T(8,128)}), f32[256,512]{1,0:T(8,128)}) %reduce-scatter.14.cloned.1.call-update) | async-done | bytes 524304 | tf_op jit(solution)/shard_map/reduce_scatter | solution.py:235
  1161.9 54.9 %reduce-scatter.20.cloned.1.call-done = f32[512,256]{1,0:T(8,128)} async-done(((f32[512,2048]{1,0:T(8,128)}), f32[512,256]{1,0:T(8,128)}) %reduce-scatter.20.cloned.1.call-update) | async-done | bytes 524304 | tf_op jit(solution)/shard_map/reduce_scatter | solution.py:238
  1216.8 91.1 %reduce-scatter.22.cloned.1.call-done = f32[256,1408]{1,0:T(8,128)} async-done(((f32[2048,1408]{1,0:T(8,128)}), f32[256,1408]{1,0:T(8,128)}) %reduce-scatter.22.cloned.1.call-update) | async-done | bytes 1441808 | tf_op jit(solution)/shard_map/reduce_scatter | solution.py:240
  1307.8 91.1 %reduce-scatter.24.cloned.1.call-done = f32[256,1408]{1,0:T(8,128)} async-done(((f32[2048,1408]{1,0:T(8,128)}), f32[256,1408]{1,0:T(8,128)}) %reduce-scatter.24.cloned.1.call-update) | async-done | bytes 1441808 | tf_op jit(solution)/shard_map/reduce_scatter | solution.py:241
  1398.9 90.8 %reduce-scatter.26.cloned.1.call-done = f32[1408,256]{1,0:T(8,128)} async-done(((f32[1408,2048]{1,0:T(8,128)}), f32[1408,256]{1,0:T(8,128)}) %reduce-scatter.26.cloned.1.call-update) | async-done | bytes 1441808 | tf_op jit(solution)/shard_map/reduce_scatter | solution.py:242
  (312 shorter events, 79.1 us)
Async XLA Ops:
  7.2 24.7 %copy-start.2 = (bf16[2,256,2048]{2,1,0:T(8,128)(2,1)S(1)}, bf16[2,256,2048]{2,1,0:T(8,128)(2,1)}, u32[]{:S(2)}) copy-start(bf16[2,256,2048]{2,1,0:T(8,128)(2,1)} %param.12) | copy-start | bytes 6291460
  7.2 14.8 copy-start.79
  7.2 71.7 %all-gather.10.cloned.1.call-start = ((), (), s32[]{:S(2)}) async-start(), calls=%async_computation.9 | async-start | bytes 2359296 | tf_op jit(solution)/shard_map/all_gather | solution.py:48
  7.9 87.7 %all-gather.12.cloned.1.call-start = ((), (), s32[]{:S(2)}) async-start(), calls=%async_computation.10 | async-start | bytes 2359296 | tf_op jit(solution)/shard_map/all_gather | solution.py:51
  8.7 248.4 %all-reduce.12.cloned.1.call-start = ((), (), s32[]{:S(2)}) async-start(), calls=%async_computation.24 | async-start | bytes 8388608 | tf_op jit(solution)/shard_map/psum | solution.py:149
  8.7 35.8 %copy-start.88 = (f32[32]{0:T(128)}, f32[32]{0:T(128)S(1)}, u32[]{:S(2)}) copy-start(f32[32]{0:T(128)S(1)} %multiply_power_fusion) | copy-start | bytes 388
  8.8 35.8 %copy-start.86 = (f32[256]{0:T(256)}, f32[256]{0:T(256)S(1)}, u32[]{:S(2)}) copy-start(f32[256]{0:T(256)S(1)} %fusion.169) | copy-start | bytes 3076
  22.0 60.9 %copy-start.82 = (f32[256]{0:T(256)}, f32[256]{0:T(256)S(1)}, u32[]{:S(2)}) copy-start(f32[256]{0:T(256)S(1)} %add_rsqrt_fusion.3) | copy-start | bytes 3076
  22.0 63.4 %copy-start.84 = (f32[256]{0:T(256)}, f32[256]{0:T(256)S(1)}, u32[]{:S(2)}) copy-start(f32[256]{0:T(256)S(1)} %add_rsqrt_fusion.1) | copy-start | bytes 3076
  43.2 7.0 copy-start.90
  66.4 25.2 %copy-start.56 = (bf16[1024,64]{0,1:T(8,128)(2,1)}, bf16[1024,64]{0,1:T(8,128)(2,1)S(1)}, u32[]{:S(2)}) copy-start(bf16[1024,64]{0,1:T(8,128)(2,1)S(1)} %all-gather.1) | copy-start | bytes 393220
  71.9 16.0 %copy-start.32 = (bf16[1,1024,64]{1,2,0:T(8,128)(2,1)}, bf16[1,1024,64]{1,2,0:T(8,128)(2,1)S(1)}, u32[]{:S(2)}) copy-start(bf16[1,1024,64]{1,2,0:T(8,128)(2,1)S(1)} %all_gather.59) | copy-start | bytes 393220
  87.9 3.7 copy-start
  87.9 3.7 copy-start.67
  89.4 4.6 copy-start.1
  95.6 3.8 copy-start.42
  95.6 3.8 copy-start.5
  101.5 199.5 %all-gather.14.cloned.1.call-start = ((), (), s32[]{:S(2)}) async-start(), calls=%async_computation.11 | async-start | bytes 6488064 | tf_op jit(solution)/shard_map/all_gather | solution.py:53
  102.1 243.9 %all-gather.16.cloned.1.call-start = ((), (), s32[]{:S(2)}) async-start(), calls=%async_computation.12 | async-start | bytes 6488064 | tf_op jit(solution)/shard_map/all_gather | solution.py:54
  102.7 289.3 %all-gather.18.cloned.1.call-start = ((), (), s32[]{:S(2)}) async-start(), calls=%async_computation.13 | async-start | bytes 6488064 | tf_op jit(solution)/shard_map/all_gather | solution.py:55
  103.2 664.6 %all-reduce.14.cloned.1.call-start = ((), (), s32[]{:S(2)}) async-start(), calls=%async_computation.25 | async-start | bytes 4194304 | tf_op jit(solution)/shard_map/psum | solution.py:158
  262.7 83.3 %copy-start.16 = (bf16[256,2048]{1,0:T(8,128)(2,1)}, bf16[256,2048]{1,0:T(8,128)(2,1)S(1)}, u32[]{:S(2)}) copy-start(bf16[256,2048]{1,0:T(8,128)(2,1)S(1)} %fusion.72) | copy-start | bytes 3145732
  392.0 6.2 copy-start.91
  398.2 207.2 %copy-start.48 = (bf16[256,1408]{1,0:T(8,128)(2,1)}, bf16[256,1408]{1,0:T(8,128)(2,1)S(1)}, u32[]{:S(2)}) copy-start(bf16[256,1408]{1,0:T(8,128)(2,1)S(1)} %get-tuple-element.37) | copy-start | bytes 2162692
  398.2 3.4 copy-start.92
  400.1 54.0 %slice-start = ((s8[5767168]{0:T(1024)(128)(4,1)}), s8[4194304]{0:T(1024)(128)(4,1)S(1)}, s32[]{:S(2)}) async-start(s8[5767168]{0:T(1024)(128)(4,1)} %bitcast.376), calls=%async_computation.26 | async-start | bytes 8388608
  401.6 52.5 %slice-start.1 = ((s8[5767168]{0:T(1024)(128)(4,1)}), s8[1572864]{0:T(1024)(128)(4,1)S(1)}, s32[]{:S(2)}) async-start(s8[5767168]{0:T(1024)(128)(4,1)} %bitcast.376), calls=%async_computation.27 | async-start | bytes 3145728
  403.4 50.6 %copy-start.17 = (bf16[2,256,2048]{2,1,0:T(8,128)(2,1)S(1)}, bf16[2,256,2048]{2,1,0:T(8,128)(2,1)}, u32[]{:S(2)}) copy-start(bf16[2,256,2048]{2,1,0:T(8,128)(2,1)} %param.13) | copy-start | bytes 6291460
  403.5 47.8 %collective-permute-start = (f32[1,256,2048]{2,1,0:T(8,128)S(1)}, f32[1,256,2048]{2,1,0:T(8,128)S(1)}, u32[]{:S(2)}, u32[]{:S(2)}) collective-permute-start(f32[1,256,2048]{2,1,0:T(8,128)S(1)} %fusion.35), channel_id=1, source_target_pairs={{0,1},{1,0},{2,3},{3,2},{4,5},{5,4},{6,7},{7,6},{8,9},{9,8},{10,11... | collective-permute-start | bytes 6291464 | tf_op jit(solution)/shard_map/ppermute | solution.py:176
  451.6 92.8 %copy-start.14 = (f32[1,256,2048]{2,1,0:T(8,128)}, f32[1,256,2048]{2,1,0:T(8,128)S(1)}, u32[]{:S(2)}) copy-start(f32[1,256,2048]{2,1,0:T(8,128)S(1)} %add.249) | copy-start | bytes 6291460
  451.6 92.8 %collective-permute-start.1 = (f32[1,256,2048]{2,1,0:T(8,128)S(1)}, f32[1,256,2048]{2,1,0:T(8,128)S(1)}, u32[]{:S(2)}, u32[]{:S(2)}) collective-permute-start(f32[1,256,2048]{2,1,0:T(8,128)S(1)} %add.249), channel_id=1, source_target_pairs={{0,2},{1,3},{2,0},{3,1},{4,6},{5,7},{6,4},{7,5},{8,10},{9,11},{10,... | collective-permute-start | bytes 6291464 | tf_op jit(solution)/shard_map/ppermute | solution.py:176
  454.1 90.3 %copy-start.10 = (f32[1,256,2048]{2,1,0:T(8,128)S(1)}, f32[1,256,2048]{2,1,0:T(8,128)}, u32[]{:S(2)}) copy-start(f32[1,256,2048]{2,1,0:T(8,128)} %copy-done.9) | copy-start | bytes 6291460
  454.1 90.3 %copy-start.11 = (f32[1,256,2048]{2,1,0:T(8,128)S(1)}, f32[1,256,2048]{2,1,0:T(8,128)}, u32[]{:S(2)}) copy-start(f32[1,256,2048]{2,1,0:T(8,128)} %get-tuple-element.48) | copy-start | bytes 6291460
  550.3 57.9 %copy-start.22 = (bf16[256,1408]{1,0:T(8,128)(2,1)}, bf16[256,1408]{1,0:T(8,128)(2,1)S(1)}, u32[]{:S(2)}) copy-start(bf16[256,1408]{1,0:T(8,128)(2,1)S(1)} %get-tuple-element.40) | copy-start | bytes 2162692
  554.0 46.7 %collective-permute-start.2 = (f32[1,256,2048]{2,1,0:T(8,128)S(1)}, f32[1,256,2048]{2,1,0:T(8,128)S(1)}, u32[]{:S(2)}, u32[]{:S(2)}) collective-permute-start(f32[1,256,2048]{2,1,0:T(8,128)S(1)} %fusion.34), channel_id=1, source_target_pairs={{0,1},{1,0},{2,3},{3,2},{4,5},{5,4},{6,7},{7,6},{8,9},{9,8},{10,11... | collective-permute-start | bytes 6291464 | tf_op jit(solution)/shard_map/ppermute | solution.py:176
  602.3 161.4 %collective-permute-start.3 = (f32[1,256,2048]{2,1,0:T(8,128)}, f32[1,256,2048]{2,1,0:T(8,128)}, u32[]{:S(2)}, u32[]{:S(2)}) collective-permute-start(f32[1,256,2048]{2,1,0:T(8,128)} %add.262), channel_id=1, source_target_pairs={{0,2},{1,3},{2,0},{3,1},{4,6},{5,7},{6,4},{7,5},{8,10},{9,11},{10,... | collective-permute-start | bytes 6291464 | tf_op jit(solution)/shard_map/ppermute | solution.py:176
  611.0 232.8 %reduce-scatter.10.cloned.1.call-start = ((), (), s32[]{:S(2)}) async-start(), calls=%async_computation.14 | async-start | bytes 655360 | tf_op jit(solution)/shard_map/reduce_scatter | solution.py:211
  767.9 10.4 copy-start.6
  780.8 8.7 copy-start.60
  789.5 5.6 copy-start.7
  789.6 5.6 copy-start.12
  806.6 5.5 copy-start.61
  806.6 5.5 copy-start.77
  812.2 6.8 copy-start.39
  812.2 6.8 copy-start.41
  821.9 46.7 %reduce-scatter.12.cloned.1.call-start = ((), (), s32[]{:S(2)}) async-start(), calls=%async_computation.15 | async-start | bytes 655360 | tf_op jit(solution)/shard_map/reduce_scatter | solution.py:211
  822.1 7.1 copy-start.35
  822.1 7.1 copy-start.37
  834.9 197.4 %all-reduce.10.cloned.1.call-start = ((), (), s32[]{:S(2)}) async-start(), calls=%async_computation.23 | async-start | bytes 8388608 | tf_op jit(solution)/shard_map/psum | solution.py:228
  838.9 30.6 %copy-start.87 = (f32[256]{0:T(256)S(1)}, f32[256]{0:T(256)}, u32[]{:S(2)}) copy-start(f32[256]{0:T(256)} %copy-done.86) | copy-start | bytes 3076
  838.9 30.6 %copy-start.89 = (f32[32]{0:T(128)S(1)}, f32[32]{0:T(128)}, u32[]{:S(2)}) copy-start(f32[32]{0:T(128)} %copy-done.88) | copy-start | bytes 388
  838.9 31.4 %copy-start.25 = (bf16[2048,64]{0,1:T(8,128)(2,1)S(1)}, bf16[2048,64]{0,1:T(8,128)(2,1)}, u32[]{:S(2)}) copy-start(bf16[2048,64]{0,1:T(8,128)(2,1)} %copy-done.24) | copy-start | bytes 786436
  869.7 4.5 copy-start.73
  869.7 4.5 copy-start.75
  877.1 191.9 %reduce-scatter.16.cloned.1.call-start = ((), (), s32[]{:S(2)}) async-start(), calls=%async_computation.17 | async-start | bytes 589824 | tf_op jit(solution)/shard_map/reduce_scatter | solution.py:236
  879.6 227.1 %reduce-scatter.18.cloned.1.call-start = ((), (), s32[]{:S(2)}) async-start(), calls=%async_computation.18 | async-start | bytes 589824 | tf_op jit(solution)/shard_map/reduce_scatter | solution.py:237
  881.5 280.4 %reduce-scatter.14.cloned.1.call-start = ((), (), s32[]{:S(2)}) async-start(), calls=%async_computation.16 | async-start | bytes 4718592 | tf_op jit(solution)/shard_map/reduce_scatter | solution.py:235
  886.3 330.5 %reduce-scatter.20.cloned.1.call-start = ((), (), s32[]{:S(2)}) async-start(), calls=%async_computation.19 | async-start | bytes 4718592 | tf_op jit(solution)/shard_map/reduce_scatter | solution.py:238
  892.4 415.4 %reduce-scatter.22.cloned.1.call-start = ((), (), s32[]{:S(2)}) async-start(), calls=%async_computation.20 | async-start | bytes 12976128 | tf_op jit(solution)/shard_map/reduce_scatter | solution.py:240
  892.7 3.4 copy-start.55
  902.2 496.7 %reduce-scatter.24.cloned.1.call-start = ((), (), s32[]{:S(2)}) async-start(), calls=%async_computation.21 | async-start | bytes 12976128 | tf_op jit(solution)/shard_map/reduce_scatter | solution.py:241
  902.3 3.3 copy-start.53
  911.8 4.2 copy-start.23
  911.8 577.9 %reduce-scatter.26.cloned.1.call-start = ((), (), s32[]{:S(2)}) async-start(), calls=%async_computation.22 | async-start | bytes 12976128 | tf_op jit(solution)/shard_map/reduce_scatter | solution.py:242
  (54 other events, 86.1 us)
Sparse Core Ops, SparseCore 0:
  9.9 31.1 all-gather.9
  43.0 28.4 all-gather.11
  101.6 155.3 all-reduce.11
  258.8 42.1 all-gather.13
  302.7 43.1 all-gather.15
  347.7 44.2 all-gather.17
  611.2 152.3 all-reduce.13
  822.0 21.8 reduce-scatter.9
  846.9 21.6 reduce-scatter.11
  877.2 155.0 all-reduce.9
  1035.9 33.0 reduce-scatter.15
  1072.6 34.1 reduce-scatter.17
  1110.7 51.1 reduce-scatter.13
  1165.6 51.0 reduce-scatter.19
  1220.7 87.1 reduce-scatter.21
  1311.8 87.1 reduce-scatter.23
  1402.9 86.8 reduce-scatter.25
